TPU v7x, 512 devices: a whole 4x4x16 slice. The times are simulated.
512 devices in a mesh: section: 16 (over z), chan: 32 (over y, x, core).
Axes of the slice: x: 4, y: 4, z: 16, core: 2. Of those that a mesh axis runs over, the one named last changes fastest.
Arguments:
- inputs: bfloat16 [4, 512, 256], P(None, 'chan'), may hold values from -6 to 6
- front: bfloat16 [16, 512, 256], P('section', 'chan'), may hold values from -6 to 6
- back: bfloat16 [16, 512, 256], P('section', 'chan'), may hold values from -6 to 6
- saved: bfloat16 [16, 4, 512, 256], P('section', None, 'chan'), may hold values from -6 to 6
- weights: bfloat16 [16, 512, 27, 512], P('section', 'chan'), may hold values from -0.1875 to 0.1875
- cotangent: bfloat16 [4, 512, 256], P(None, 'chan'), may hold values from -6 to 6
Outputs:
- acts: bfloat16 [16, 4, 512, 256], P('section', None, 'chan')
- grads: bfloat16 [16, 4, 512, 256], P('section', None, 'chan')
- weight_grads: float32 [16, 512, 27, 512], P('section', 'chan')
All inputs are finite; a program needn't handle non-finite values.
Results may differ from a plain program's by a relative error of at most 0.035.
Values may be sent and summed in bfloat16 or wider, within the bound.
No kernel may reach another device: no remote copies, remote signals or barrier semaphores. Data moves between devices by JAX's collectives and lax.ppermute only.
A program may use at most 128 MiB of HBM per device.

v0:
```python
import jax
import jax.numpy as jnp
from jax import lax
from jax.sharding import PartitionSpec as P

SX = 4
SY = 8
SZ = 8
TAP_OFFSETS = [(i - 1, j - 1, l - 1) for i in range(3) for j in range(3) for l in range(3)]


def from_behind(value, axis, steps):
    count = lax.axis_size(axis)
    first, last = (max(0, -steps), min(count, count - steps))
    return lax.ppermute(value, axis, [(source, source + steps) for source in range(first, last)])


def shifted_view(values, offset):
    cell_count = SX * SY * SZ
    margin = SY * SZ + SZ + 1
    lead = values.ndim - 1
    padded = jnp.pad(values, [(0, 0)] * lead + [(margin, margin)])
    delta = offset[0] * SY * SZ + offset[1] * SZ + offset[2]
    moved = padded[..., margin + delta : margin + delta + cell_count]
    index = jnp.arange(cell_count, dtype=jnp.int32)
    first_pos = index // (SY * SZ) + offset[0]
    second_pos = index // SZ % SY + offset[1]
    third_pos = index % SZ + offset[2]
    inside = (
        (first_pos >= 0)
        & (first_pos < SX)
        & (second_pos >= 0)
        & (second_pos < SY)
        & (third_pos >= 0)
        & (third_pos < SZ)
    )
    return jnp.where(inside, moved, jnp.zeros_like(moved))


def tap_sum(taps):
    accum = shifted_view(taps[..., 0, :], TAP_OFFSETS[0])
    for index in range(1, 27):
        accum = accum + shifted_view(taps[..., index, :], TAP_OFFSETS[index])
    return accum


def tap_spread(values):
    return jnp.stack([shifted_view(values, (-o[0], -o[1], -o[2])) for o in TAP_OFFSETS], axis=-2)


def silu_slope(pre):
    logistic = jax.nn.sigmoid(pre)
    return logistic * (1.0 + pre * (1.0 - logistic))


def body(inputs, front, back, saved, weights, cotangent):
    section_count = lax.axis_size("section")
    section_index = lax.axis_index("section")
    first_section = section_index == 0
    last_section = section_index == section_count - 1
    round_count, own_filters, cell_count = inputs.shape
    channels = weights.shape[3]
    weight_rows = weights.reshape(own_filters * 27, channels)
    acts_list = []
    grads_list = []
    filter_grad = jnp.zeros((own_filters * 27, channels), jnp.float32)
    forward_recv = front[0]
    backward_recv = back[0]
    for round_index in range(round_count):
        layer_in = jnp.where(first_section, inputs[round_index], forward_recv)
        taps = jnp.dot(
            weight_rows,
            lax.all_gather(layer_in, "chan", axis=0, tiled=True),
            preferred_element_type=jnp.float32,
        )
        pre = tap_sum(taps.reshape(own_filters, 27, cell_count))
        layer_out = jax.nn.silu(pre).astype(jnp.bfloat16)
        acts_list.append(layer_out)
        if round_index + 1 < round_count:
            forward_recv = from_behind(layer_out, "section", 1)
        whole_in = lax.all_gather(saved[0, round_index], "chan", axis=0, tiled=True)
        back_taps = jnp.dot(weight_rows, whole_in, preferred_element_type=jnp.float32)
        pre_back = tap_sum(back_taps.reshape(own_filters, 27, cell_count))
        grad_out = jnp.where(last_section, cotangent[round_index], backward_recv)
        dpre = (grad_out.astype(jnp.float32) * silu_slope(pre_back)).astype(jnp.bfloat16)
        spread = tap_spread(dpre).reshape(own_filters * 27, cell_count)
        grad_in = lax.psum_scatter(
            lax.dot_general(
                weight_rows, spread, (((0,), (0,)), ((), ())), preferred_element_type=jnp.float32
            ).astype(jnp.bfloat16),
            "chan",
            scatter_dimension=0,
            tiled=True,
        )
        filter_grad = filter_grad + lax.dot_general(
            spread, whole_in, (((1,), (1,)), ((), ())), preferred_element_type=jnp.float32
        )
        grads_list.append(grad_in)
        if round_index + 1 < round_count:
            backward_recv = from_behind(grad_in, "section", -1)
    acts = jnp.stack(acts_list, axis=0)[None]
    grads = jnp.stack(grads_list, axis=0)[None]
    return (acts, grads, filter_grad.reshape(1, own_filters, 27, channels))


def solution(mesh):
    return jax.shard_map(
        body,
        mesh=mesh,
        in_specs=(
            P(None, "chan", None),
            P("section", "chan", None),
            P("section", "chan", None),
            P("section", None, "chan", None),
            P("section", "chan", None, None),
            P(None, "chan", None),
        ),
        out_specs=(
            P("section", None, "chan", None),
            P("section", None, "chan", None),
            P("section", "chan", None, None),
        ),
        check_vma=False,
    )
```

profile of v0, /device:TPU:2, one launch (start us, length us, event | category | flops | bytes accessed | tf_op | source)
XLA Modules:
  0.0 543.6 jit_solution(12856307479175917620)
XLA Ops:
  8.0 27.6 %all-gather.1 = bf16[1,1,512,256]{3,2,1,0:T(8,128)(2,1)S(1)} all-gather(bf16[1,1,16,256]{3,2,1,0:T(8,128)(2,1)S(1)} %get-tuple-element.222), channel_id=3, replica_groups=mesh['section'=16,'chan'=32] {'chan'}, dimensions={2}, use_global_device_ids=true | all-gather | bytes 270336 | tf_op jit(solution)/shard_map/all_gather | solution.py:81
  35.6 1.5 fusion.4
  42.5 1.1 fusion
  44.3 22.0 %all-gather = bf16[1,512,256]{2,1,0:T(8,128)(2,1)S(1)} all-gather(bf16[1,16,256]{2,1,0:T(8,128)(2,1)S(1)} %slice_select_fusion), channel_id=2, replica_groups=mesh['section'=16,'chan'=32] {'chan'}, dimensions={1}, use_global_device_ids=true | all-gather | bytes 270336 | tf_op jit(solution)/shard_map/all_gather | solution.py:73
  67.6 2.0 collective-permute-start
  69.6 23.9 %all-gather.2 = bf16[1,1,512,256]{3,2,1,0:T(8,128)(2,1)S(1)} all-gather(bf16[1,1,16,256]{3,2,1,0:T(8,128)(2,1)S(1)} %get-tuple-element.223), channel_id=4, replica_groups=mesh['section'=16,'chan'=32] {'chan'}, dimensions={2}, use_global_device_ids=true | all-gather | bytes 270336 | tf_op jit(solution)/shard_map/all_gather | solution.py:81
  95.7 22.7 %all-gather.3 = bf16[1,1,512,256]{3,2,1,0:T(8,128)(2,1)S(1)} all-gather(bf16[1,1,16,256]{3,2,1,0:T(8,128)(2,1)S(1)} %get-tuple-element.225), channel_id=5, replica_groups=mesh['section'=16,'chan'=32] {'chan'}, dimensions={2}, use_global_device_ids=true | all-gather | bytes 270336 | tf_op jit(solution)/shard_map/all_gather | solution.py:81
  119.5 24.2 %all-gather.4 = bf16[1,1,512,256]{3,2,1,0:T(8,128)(2,1)S(1)} all-gather(bf16[1,1,16,256]{3,2,1,0:T(8,128)(2,1)S(1)} %get-tuple-element.224), channel_id=6, replica_groups=mesh['section'=16,'chan'=32] {'chan'}, dimensions={2}, use_global_device_ids=true | all-gather | bytes 270336 | tf_op jit(solution)/shard_map/all_gather | solution.py:81
  145.5 22.6 %all_gather.25 = bf16[512,256]{1,0:T(8,128)(2,1)S(1)} all-gather(bf16[16,256]{1,0:T(8,128)(2,1)S(1)} %bitcast_select_fusion.5), channel_id=1, replica_groups=mesh['section'=16,'chan'=32] {'chan'}, dimensions={0}, use_global_device_ids=true | all-gather | bytes 270336 | tf_op jit(solution)/shard_map/all_gather | solution.py:73
  170.2 3.8 collective-permute-start.1
  176.1 23.8 %all_gather.26 = bf16[512,256]{1,0:T(8,128)(2,1)S(1)} all-gather(bf16[16,256]{1,0:T(8,128)(2,1)S(1)} %bitcast_select_fusion.4), channel_id=1, replica_groups=mesh['section'=16,'chan'=32] {'chan'}, dimensions={0}, use_global_device_ids=true | all-gather | bytes 270336 | tf_op jit(solution)/shard_map/all_gather | solution.py:73
  200.9 1.3 collective-permute-start.3
  202.7 4.8 collective-permute-start.2
  213.3 22.7 %all_gather.27 = bf16[512,256]{1,0:T(8,128)(2,1)S(1)} all-gather(bf16[16,256]{1,0:T(8,128)(2,1)S(1)} %bitcast_select_fusion.3), channel_id=1, replica_groups=mesh['section'=16,'chan'=32] {'chan'}, dimensions={0}, use_global_device_ids=true | all-gather | bytes 270336 | tf_op jit(solution)/shard_map/all_gather | solution.py:73
  236.3 78.7 %reduce-scatter.7.cloned.1.call-done = bf16[16,256]{1,0:T(8,128)(2,1)} async-done(((bf16[512,256]{1,0:T(8,128)(2,1)}), bf16[16,256]{1,0:T(8,128)(2,1)}) %reduce-scatter.7.cloned.1.call-update) | async-done | bytes 8208 | tf_op jit(solution)/shard_map/reduce_scatter | solution.py:87
  315.1 1.5 collective-permute-start.4
  317.8 3.0 collective-permute-done.4
  321.6 1.1 multiply_convert_fusion.1
  336.8 88.7 %reduce-scatter.9.cloned.1.call-done = bf16[16,256]{1,0:T(8,128)(2,1)} async-done(((bf16[512,256]{1,0:T(8,128)(2,1)}), bf16[16,256]{1,0:T(8,128)(2,1)}) %reduce-scatter.9.cloned.1.call-update) | async-done | bytes 8208 | tf_op jit(solution)/shard_map/reduce_scatter | solution.py:87
  425.5 1.3 collective-permute-start.5
  427.4 3.9 collective-permute-done.5
  437.0 1.4 copy.461
  438.5 97.3 %reduce-scatter.11.cloned.1.call-done = bf16[16,256]{1,0:T(8,128)(2,1)} async-done(((bf16[512,256]{1,0:T(8,128)(2,1)}), bf16[16,256]{1,0:T(8,128)(2,1)}) %reduce-scatter.11.cloned.1.call-update) | async-done | bytes 8208 | tf_op jit(solution)/shard_map/reduce_scatter | solution.py:87
  535.8 1.3 maximum_bitcast_fusion.1
  (615 shorter events, 44.4 us)
Async XLA Ops:
  7.2 193.7 %reduce-scatter.5.cloned.1.call-start = ((), (), s32[]{:S(2)}) async-start(), calls=%async_computation.4 | async-start | bytes 270336 | tf_op jit(solution)/shard_map/reduce_scatter | solution.py:87
  37.4 29.8 %copy-start.55 = (pred[256]{0:T(512)(128)(4,1)}, pred[256]{0:T(512)(128)(4,1)S(1)}, u32[]{:S(2)}) copy-start(pred[256]{0:T(512)(128)(4,1)S(1)} %get-tuple-element.253) | copy-start | bytes 772
  37.4 29.8 %copy-start.58 = (pred[256]{0:T(512)(128)(4,1)}, pred[256]{0:T(512)(128)(4,1)S(1)}, u32[]{:S(2)}) copy-start(pred[256]{0:T(512)(128)(4,1)S(1)} %get-tuple-element.252) | copy-start | bytes 772
  37.5 29.8 %copy-start.49 = (pred[256]{0:T(512)(128)(4,1)}, pred[256]{0:T(512)(128)(4,1)S(1)}, u32[]{:S(2)}) copy-start(pred[256]{0:T(512)(128)(4,1)S(1)} %get-tuple-element.255) | copy-start | bytes 772
  37.5 29.8 %copy-start.52 = (pred[256]{0:T(512)(128)(4,1)}, pred[256]{0:T(512)(128)(4,1)S(1)}, u32[]{:S(2)}) copy-start(pred[256]{0:T(512)(128)(4,1)S(1)} %get-tuple-element.254) | copy-start | bytes 772
  37.5 29.7 %copy-start.43 = (pred[256]{0:T(512)(128)(4,1)}, pred[256]{0:T(512)(128)(4,1)S(1)}, u32[]{:S(2)}) copy-start(pred[256]{0:T(512)(128)(4,1)S(1)} %get-tuple-element.257) | copy-start | bytes 772
  37.5 29.7 %copy-start.46 = (pred[256]{0:T(512)(128)(4,1)}, pred[256]{0:T(512)(128)(4,1)S(1)}, u32[]{:S(2)}) copy-start(pred[256]{0:T(512)(128)(4,1)S(1)} %get-tuple-element.256) | copy-start | bytes 772
  37.5 29.7 %copy-start.37 = (pred[256]{0:T(512)(128)(4,1)}, pred[256]{0:T(512)(128)(4,1)S(1)}, u32[]{:S(2)}) copy-start(pred[256]{0:T(512)(128)(4,1)S(1)} %get-tuple-element.259) | copy-start | bytes 772
  37.5 29.7 %copy-start.40 = (pred[256]{0:T(512)(128)(4,1)}, pred[256]{0:T(512)(128)(4,1)S(1)}, u32[]{:S(2)}) copy-start(pred[256]{0:T(512)(128)(4,1)S(1)} %get-tuple-element.258) | copy-start | bytes 772
  37.6 29.7 %copy-start.31 = (pred[256]{0:T(512)(128)(4,1)}, pred[256]{0:T(512)(128)(4,1)S(1)}, u32[]{:S(2)}) copy-start(pred[256]{0:T(512)(128)(4,1)S(1)} %get-tuple-element.261) | copy-start | bytes 772
  37.6 29.7 %copy-start.34 = (pred[256]{0:T(512)(128)(4,1)}, pred[256]{0:T(512)(128)(4,1)S(1)}, u32[]{:S(2)}) copy-start(pred[256]{0:T(512)(128)(4,1)S(1)} %get-tuple-element.260) | copy-start | bytes 772
  43.6 271.5 %reduce-scatter.7.cloned.1.call-start = ((), (), s32[]{:S(2)}) async-start(), calls=%async_computation.5 | async-start | bytes 270336 | tf_op jit(solution)/shard_map/reduce_scatter | solution.py:87
  67.6 77.9 %collective-permute-start = (bf16[16,256]{1,0:T(8,128)(2,1)S(1)}, bf16[16,256]{1,0:T(8,128)(2,1)S(1)}, u32[]{:S(2)}, u32[]{:S(2)}) collective-permute-start(bf16[16,256]{1,0:T(8,128)(2,1)S(1)} %multiply_convert_fusion.6), channel_id=1, source_target_pairs={{0,32},{32,64},{64,96},{96,128},{128,160},{160,192},{192,224},{224... | collective-permute-start | bytes 24584 | tf_op jit(solution)/shard_map/ppermute | solution.py:15
  144.0 30.0 %copy-start.1 = (f32[16,27,256]{2,0,1:T(8,128)}, f32[16,27,256]{2,0,1:T(8,128)S(1)}, u32[]{:S(2)}) copy-start(f32[16,27,256]{2,0,1:T(8,128)S(1)} %fusion.6) | copy-start | bytes 1327108
  170.2 5.2 collective-permute-start.1
  200.9 6.6 %collective-permute-start.3 = (bf16[16,256]{1,0:T(8,128)(2,1)}, bf16[16,256]{1,0:T(8,128)(2,1)S(1)}, u32[]{:S(2)}, u32[]{:S(2)}) collective-permute-start(bf16[16,256]{1,0:T(8,128)(2,1)} %reduce-scatter.5.cloned.1.call-done), channel_id=1, source_target_pairs={{32,0},{64,32},{96,64},{128,96},{160,128},{192,160},{224,192},{256... | collective-permute-start | bytes 24584 | tf_op jit(solution)/shard_map/ppermute | solution.py:15
  202.7 9.9 %collective-permute-start.2 = (bf16[16,256]{1,0:T(8,128)(2,1)S(1)}, bf16[16,256]{1,0:T(8,128)(2,1)S(1)}, u32[]{:S(2)}, u32[]{:S(2)}) collective-permute-start(bf16[16,256]{1,0:T(8,128)(2,1)S(1)} %multiply_convert_fusion.4), channel_id=1, source_target_pairs={{0,32},{32,64},{64,96},{96,128},{128,160},{160,192},{192,224},{224... | collective-permute-start | bytes 24584 | tf_op jit(solution)/shard_map/ppermute | solution.py:15
  212.5 213.0 %reduce-scatter.9.cloned.1.call-start = ((), (), s32[]{:S(2)}) async-start(), calls=%async_computation.6 | async-start | bytes 270336 | tf_op jit(solution)/shard_map/reduce_scatter | solution.py:87
  315.1 5.7 %collective-permute-start.4 = (bf16[16,256]{1,0:T(8,128)(2,1)}, bf16[16,256]{1,0:T(8,128)(2,1)S(1)}, u32[]{:S(2)}, u32[]{:S(2)}) collective-permute-start(bf16[16,256]{1,0:T(8,128)(2,1)} %reduce-scatter.7.cloned.1.call-done), channel_id=1, source_target_pairs={{32,0},{64,32},{96,64},{128,96},{160,128},{192,160},{224,192},{256... | collective-permute-start | bytes 24584 | tf_op jit(solution)/shard_map/ppermute | solution.py:15
  326.0 209.8 %reduce-scatter.11.cloned.1.call-start = ((), (), s32[]{:S(2)}) async-start(), calls=%async_computation.7 | async-start | bytes 270336 | tf_op jit(solution)/shard_map/reduce_scatter | solution.py:87
  425.5 5.7 %collective-permute-start.5 = (bf16[16,256]{1,0:T(8,128)(2,1)}, bf16[16,256]{1,0:T(8,128)(2,1)S(1)}, u32[]{:S(2)}, u32[]{:S(2)}) collective-permute-start(bf16[16,256]{1,0:T(8,128)(2,1)} %reduce-scatter.9.cloned.1.call-done), channel_id=1, source_target_pairs={{32,0},{64,32},{96,64},{128,96},{160,128},{192,160},{224,192},{256... | collective-permute-start | bytes 24584 | tf_op jit(solution)/shard_map/ppermute | solution.py:15
  437.0 98.8 %copy-start.156 = (bf16[16,256]{1,0:T(8,128)(2,1)S(1)}, bf16[16,256]{1,0:T(8,128)(2,1)}, u32[]{:S(2)}) copy-start(bf16[16,256]{1,0:T(8,128)(2,1)} %reduce-scatter.5.cloned.1.call-done) | copy-start | bytes 24580
  437.0 98.8 %copy-start.157 = (bf16[16,256]{1,0:T(8,128)(2,1)S(1)}, bf16[16,256]{1,0:T(8,128)(2,1)}, u32[]{:S(2)}) copy-start(bf16[16,256]{1,0:T(8,128)(2,1)} %reduce-scatter.7.cloned.1.call-done) | copy-start | bytes 24580
  437.0 98.8 %copy-start.158 = (bf16[16,256]{1,0:T(8,128)(2,1)S(1)}, bf16[16,256]{1,0:T(8,128)(2,1)}, u32[]{:S(2)}) copy-start(bf16[16,256]{1,0:T(8,128)(2,1)} %reduce-scatter.9.cloned.1.call-done) | copy-start | bytes 24580
  (145 other events, 739.1 us)
Sparse Core Ops, SparseCore 0:
  43.7 99.4 reduce-scatter.4
  212.6 102.4 reduce-scatter.6
  326.1 99.3 reduce-scatter.8
  436.4 99.3 reduce-scatter.10
where the time goes:
time: 547 us; the launch traced here: 544 us
  waiting for transfers between devices  272 us (50%)
  blocking collectives  190 us (35%)
  local copies, waits for them, and re-layouts  24.7 us (5%)
  between operations  17 us (3%)
  other arithmetic  16.3 us (3%)
  starting transfers between devices  14.9 us (3%)
  matrix products  8.87 us (2%)
    reduce_scatter x4, waiting for transfers between devices, body(): lax.psum_scatter(lax.dot_general(weight_rows, spread, (((0,), (0,)), ((),...  265 us
    all_gather x4, blocking collectives, body(): whole_in = lax.all_gather(saved[0, round_index], 'chan', axis=0, tiled=True)  98.4 us
    all_gather x4, blocking collectives, body(): lax.all_gather(layer_in, 'chan', axis=0, tiled=True)  91.1 us
    unnamed x398, local copies, waits for them, and re-layouts  15.7 us
    ppermute x6, starting transfers between devices, from_behind(): lax.ppermute(value, axis, [(source, source + steps) for source in range(f...  14.7 us
  transfers between devices with their start and end apart: 10, of which 6 were waited for; matrix products, arithmetic and copies ran while one was open for 3% of the time, Pallas kernels for 0%

commit v1 on v0

--- a/solution.py
+++ b/solution.py
@@ -78,7 +78,9 @@
         acts_list.append(layer_out)
         if round_index + 1 < round_count:
             forward_recv = from_behind(layer_out, "section", 1)
-        whole_in = lax.all_gather(saved[0, round_index], "chan", axis=0, tiled=True)
+        block = saved[0, round_index]
+        sent = jnp.stack([block] * lax.axis_size("chan"))
+        whole_in = jnp.concatenate(lax.all_to_all(sent, "chan", 0, 0), axis=0)
         back_taps = jnp.dot(weight_rows, whole_in, preferred_element_type=jnp.float32)
         pre_back = tap_sum(back_taps.reshape(own_filters, 27, cell_count))
         grad_out = jnp.where(last_section, cotangent[round_index], backward_recv)

time: 547 us -> 600 us (1.097)
  waiting for transfers between devices: 272 us -> 414 us
  blocking collectives: 190 us -> 98.7 us
  starting transfers between devices: 14.9 us -> 35 us
  local copies, waits for them, and re-layouts: 24.7 us -> 13.8 us
    reduce_scatter x4, waiting for transfers between devices: 265 us -> 383 us  [body(): lax.psum_scatter(lax.dot_general(weight_rows, spread, (((0,), (0,)), ((),...]
    all_gather x4 -> x0, blocking collectives: 98.4 us -> none  [body(): whole_in = lax.all_gather(saved[0, round_index], 'chan', axis=0, tiled=True)]
    all_to_all x0 -> x4, starting transfers between devices: none -> 21.3 us  [body(): whole_in = jnp.concatenate(lax.all_to_all(sent, 'chan', 0, 0), axis=0)]
    all_to_all x0 -> x4, waiting for transfers between devices: none -> 16 us  [body(): whole_in = jnp.concatenate(lax.all_to_all(sent, 'chan', 0, 0), axis=0)]
    unnamed x398 -> x186, local copies, waits for them, and re-layouts: 15.7 us -> 5.75 us
    ppermute x6, waiting for transfers between devices: 7.58 us -> 15.4 us  [from_behind(): lax.ppermute(value, axis, [(source, source + steps) for source in range(f...]
    all_gather x4, blocking collectives: 91.1 us -> 98.7 us  [body(): lax.all_gather(layer_in, 'chan', axis=0, tiled=True)]
  transfers between devices with their start and end apart: 10 -> 14, of which waited for: 6 -> 12; matrix products, arithmetic and copies ran while one was open for 3% -> 2% of each run, Pallas kernels for 0% -> 0%
where the time goes in v1:
time: 600 us; the launch traced here: 599 us
  waiting for transfers between devices  414 us (69%)
  blocking collectives  98.7 us (16%)
  starting transfers between devices  35 us (6%)
  between operations  15.9 us (3%)
  local copies, waits for them, and re-layouts  13.8 us (2%)
  other arithmetic  13.3 us (2%)
  matrix products  7.89 us (1%)
    reduce_scatter x4, waiting for transfers between devices, body(): lax.psum_scatter(lax.dot_general(weight_rows, spread, (((0,), (0,)), ((),...  383 us
    all_gather x4, blocking collectives, body(): lax.all_gather(layer_in, 'chan', axis=0, tiled=True)  98.7 us
    all_to_all x4, starting transfers between devices, body(): whole_in = jnp.concatenate(lax.all_to_all(sent, 'chan', 0, 0), axis=0)  21.3 us
    all_to_all x4, waiting for transfers between devices, body(): whole_in = jnp.concatenate(lax.all_to_all(sent, 'chan', 0, 0), axis=0)  16 us
    ppermute x6, waiting for transfers between devices, from_behind(): lax.ppermute(value, axis, [(source, source + steps) for source in range(f...  15.4 us
    ppermute x6, starting transfers between devices, from_behind(): lax.ppermute(value, axis, [(source, source + steps) for source in range(f...  13.5 us
  transfers between devices with their start and end apart: 14, of which 12 were waited for; matrix products, arithmetic and copies ran while one was open for 2% of the time, Pallas kernels for 0%

profile of v1, /device:TPU:2, one launch (start us, length us, event | category | flops | bytes accessed | tf_op | source)
XLA Modules:
  0.0 598.9 jit_solution(17991581174404390956)
XLA Ops:
  9.4 27.6 %all-gather = bf16[1,512,256]{2,1,0:T(8,128)(2,1)S(1)} all-gather(bf16[1,16,256]{2,1,0:T(8,128)(2,1)S(1)} %slice_select_fusion), channel_id=2, replica_groups=mesh['section'=16,'chan'=32] {'chan'}, dimensions={1}, use_global_device_ids=true | all-gather | bytes 270336 | tf_op jit(solution)/shard_map/all_gather | solution.py:73
  39.4 1.3 collective-permute-done
  40.8 22.8 %all_gather.13 = bf16[512,256]{1,0:T(8,128)(2,1)S(1)} all-gather(bf16[16,256]{1,0:T(8,128)(2,1)S(1)} %bitcast_select_fusion.5), channel_id=1, replica_groups=mesh['section'=16,'chan'=32] {'chan'}, dimensions={0}, use_global_device_ids=true | all-gather | bytes 270336 | tf_op jit(solution)/shard_map/all_gather | solution.py:73
  64.8 4.2 collective-permute-start.1
  69.0 1.3 collective-permute-done.1
  70.4 23.9 %all_gather.14 = bf16[512,256]{1,0:T(8,128)(2,1)S(1)} all-gather(bf16[16,256]{1,0:T(8,128)(2,1)S(1)} %bitcast_select_fusion.4), channel_id=1, replica_groups=mesh['section'=16,'chan'=32] {'chan'}, dimensions={0}, use_global_device_ids=true | all-gather | bytes 270336 | tf_op jit(solution)/shard_map/all_gather | solution.py:73
  95.5 4.2 collective-permute-start.2
  100.4 5.6 all-to-all-start
  106.0 24.5 %all_gather.15 = bf16[512,256]{1,0:T(8,128)(2,1)S(1)} all-gather(bf16[16,256]{1,0:T(8,128)(2,1)S(1)} %bitcast_select_fusion.3), channel_id=1, replica_groups=mesh['section'=16,'chan'=32] {'chan'}, dimensions={0}, use_global_device_ids=true | all-gather | bytes 270336 | tf_op jit(solution)/shard_map/all_gather | solution.py:73
  133.1 5.8 all-to-all-start.1
  143.7 2.9 all-to-all-done.1
  147.3 5.0 all-to-all-start.2
  153.8 6.4 %all-to-all-done.2 = bf16[32,16,256]{2,1,0:T(8,128)(2,1)S(1)} async-done(((bf16[32,16,256]{2,1,0:T(8,128)(2,1)}), bf16[32,16,256]{2,1,0:T(8,128)(2,1)S(1)}, u32[]{:S(2)}, u32[]{:S(2)}) %all-to-all-start.2) | async-done | bytes 262176 | tf_op jit(solution)/shard_map/all_to_all | solution.py:83
  160.8 5.0 all-to-all-start.3
  166.8 6.8 %all-to-all-done.3 = bf16[32,16,256]{2,1,0:T(8,128)(2,1)S(1)} async-done(((bf16[32,16,256]{2,1,0:T(8,128)(2,1)}), bf16[32,16,256]{2,1,0:T(8,128)(2,1)S(1)}, u32[]{:S(2)}, u32[]{:S(2)}) %all-to-all-start.3) | async-done | bytes 262176 | tf_op jit(solution)/shard_map/all_to_all | solution.py:83
  173.9 88.4 %reduce-scatter.5.cloned.1.call-done = bf16[16,256]{1,0:T(8,128)(2,1)} async-done(((bf16[512,256]{1,0:T(8,128)(2,1)}), bf16[16,256]{1,0:T(8,128)(2,1)}) %reduce-scatter.5.cloned.1.call-update) | async-done | bytes 8208 | tf_op jit(solution)/shard_map/reduce_scatter | solution.py:89
  263.8 4.3 collective-permute-done.3
  273.2 98.8 %reduce-scatter.7.cloned.1.call-done = bf16[16,256]{1,0:T(8,128)(2,1)} async-done(((bf16[512,256]{1,0:T(8,128)(2,1)}), bf16[16,256]{1,0:T(8,128)(2,1)}) %reduce-scatter.7.cloned.1.call-update) | async-done | bytes 8208 | tf_op jit(solution)/shard_map/reduce_scatter | solution.py:89
  373.3 4.4 collective-permute-done.4
  382.5 98.3 %reduce-scatter.9.cloned.1.call-done = bf16[16,256]{1,0:T(8,128)(2,1)} async-done(((bf16[512,256]{1,0:T(8,128)(2,1)}), bf16[16,256]{1,0:T(8,128)(2,1)}) %reduce-scatter.9.cloned.1.call-update) | async-done | bytes 8208 | tf_op jit(solution)/shard_map/reduce_scatter | solution.py:89
  482.6 3.9 collective-permute-done.5
  492.3 1.4 copy.461
  493.7 97.3 %reduce-scatter.11.cloned.1.call-done = bf16[16,256]{1,0:T(8,128)(2,1)} async-done(((bf16[512,256]{1,0:T(8,128)(2,1)}), bf16[16,256]{1,0:T(8,128)(2,1)}) %reduce-scatter.11.cloned.1.call-update) | async-done | bytes 8208 | tf_op jit(solution)/shard_map/reduce_scatter | solution.py:89
  591.1 1.3 maximum_bitcast_fusion.1
  (411 shorter events, 37.6 us)
Async XLA Ops:
  38.1 2.6 collective-permute-start
  64.8 5.5 collective-permute-start.1
  95.5 10.5 %collective-permute-start.2 = (bf16[16,256]{1,0:T(8,128)(2,1)S(1)}, bf16[16,256]{1,0:T(8,128)(2,1)S(1)}, u32[]{:S(2)}, u32[]{:S(2)}) collective-permute-start(bf16[16,256]{1,0:T(8,128)(2,1)S(1)} %multiply_convert_fusion.4), channel_id=1, source_target_pairs={{0,32},{32,64},{64,96},{96,128},{128,160},{160,192},{192,224},{224... | collective-permute-start | bytes 24584 | tf_op jit(solution)/shard_map/ppermute | solution.py:15
  100.4 32.0 %all-to-all-start = ((bf16[32,16,256]{2,1,0:T(8,128)(2,1)}), bf16[32,16,256]{2,1,0:T(8,128)(2,1)S(1)}, u32[]{:S(2)}, u32[]{:S(2)}) async-start(bf16[32,16,256]{2,1,0:T(8,128)(2,1)} %stack.383), calls=%async_computation | async-start | bytes 524288 | tf_op jit(solution)/shard_map/all_to_all | solution.py:83
  131.8 7.1 %copy-start = (bf16[1,16,27,512]{3,1,2,0:T(8,128)(2,1)S(1)}, bf16[1,16,27,512]{3,1,2,0:T(8,128)(2,1)}, u32[]{:S(2)}) copy-start(bf16[1,16,27,512]{3,1,2,0:T(8,128)(2,1)} %param.10) | copy-start | bytes 1327108
  133.1 13.5 %all-to-all-start.1 = ((bf16[32,16,256]{2,1,0:T(8,128)(2,1)}), bf16[32,16,256]{2,1,0:T(8,128)(2,1)S(1)}, u32[]{:S(2)}, u32[]{:S(2)}) async-start(bf16[32,16,256]{2,1,0:T(8,128)(2,1)} %stack.413), calls=%async_computation.2 | async-start | bytes 524288 | tf_op jit(solution)/shard_map/all_to_all | solution.py:83
  143.7 8.6 %copy-start.1 = (bf16[432,256]{1,0:T(8,128)(2,1)}, bf16[432,256]{1,0:T(8,128)(2,1)S(1)}, u32[]{:S(2)}) copy-start(bf16[432,256]{1,0:T(8,128)(2,1)S(1)} %reshape.80) | copy-start | bytes 663556
  147.3 12.8 %all-to-all-start.2 = ((bf16[32,16,256]{2,1,0:T(8,128)(2,1)}), bf16[32,16,256]{2,1,0:T(8,128)(2,1)S(1)}, u32[]{:S(2)}, u32[]{:S(2)}) async-start(bf16[32,16,256]{2,1,0:T(8,128)(2,1)} %stack.443), calls=%async_computation.4 | async-start | bytes 524288 | tf_op jit(solution)/shard_map/all_to_all | solution.py:83
  152.3 110.0 %reduce-scatter.5.cloned.1.call-start = ((), (), s32[]{:S(2)}) async-start(), calls=%async_computation.8 | async-start | bytes 270336 | tf_op jit(solution)/shard_map/reduce_scatter | solution.py:89
  160.8 12.8 %all-to-all-start.3 = ((bf16[32,16,256]{2,1,0:T(8,128)(2,1)}), bf16[32,16,256]{2,1,0:T(8,128)(2,1)S(1)}, u32[]{:S(2)}, u32[]{:S(2)}) async-start(bf16[32,16,256]{2,1,0:T(8,128)(2,1)} %stack.473), calls=%async_computation.6 | async-start | bytes 524288 | tf_op jit(solution)/shard_map/all_to_all | solution.py:83
  165.8 206.1 %reduce-scatter.7.cloned.1.call-start = ((), (), s32[]{:S(2)}) async-start(), calls=%async_computation.9 | async-start | bytes 270336 | tf_op jit(solution)/shard_map/reduce_scatter | solution.py:89
  173.9 207.4 %copy-start.3 = (f32[16,27,256]{2,0,1:T(8,128)}, f32[16,27,256]{2,0,1:T(8,128)S(1)}, u32[]{:S(2)}) copy-start(f32[16,27,256]{2,0,1:T(8,128)S(1)} %fusion.645) | copy-start | bytes 1327108
  262.3 5.7 collective-permute-start.3
  263.6 4.5 copy-start.33
  272.3 208.4 %reduce-scatter.9.cloned.1.call-start = ((), (), s32[]{:S(2)}) async-start(), calls=%async_computation.10 | async-start | bytes 270336 | tf_op jit(solution)/shard_map/reduce_scatter | solution.py:89
  372.0 5.7 collective-permute-start.4
  381.2 209.8 %reduce-scatter.11.cloned.1.call-start = ((), (), s32[]{:S(2)}) async-start(), calls=%async_computation.11 | async-start | bytes 270336 | tf_op jit(solution)/shard_map/reduce_scatter | solution.py:89
  480.8 5.7 collective-permute-start.5
  482.1 4.5 copy-start.7
  482.1 4.5 copy-start.8
  482.1 4.5 copy-start.9
  492.3 98.8 %copy-start.50 = (bf16[16,256]{1,0:T(8,128)(2,1)S(1)}, bf16[16,256]{1,0:T(8,128)(2,1)}, u32[]{:S(2)}) copy-start(bf16[16,256]{1,0:T(8,128)(2,1)} %reduce-scatter.5.cloned.1.call-done) | copy-start | bytes 24580
  492.3 98.8 %copy-start.51 = (bf16[16,256]{1,0:T(8,128)(2,1)S(1)}, bf16[16,256]{1,0:T(8,128)(2,1)}, u32[]{:S(2)}) copy-start(bf16[16,256]{1,0:T(8,128)(2,1)} %reduce-scatter.7.cloned.1.call-done) | copy-start | bytes 24580
  492.3 98.8 %copy-start.52 = (bf16[16,256]{1,0:T(8,128)(2,1)S(1)}, bf16[16,256]{1,0:T(8,128)(2,1)}, u32[]{:S(2)}) copy-start(bf16[16,256]{1,0:T(8,128)(2,1)} %reduce-scatter.9.cloned.1.call-done) | copy-start | bytes 24580
  (43 other events, 154.7 us)
Sparse Core Ops, SparseCore 0:
  157.5 104.8 reduce-scatter.4
  272.5 99.4 reduce-scatter.6
  381.4 99.3 reduce-scatter.8
  491.6 99.3 reduce-scatter.10
